TPU v7x, 32 devices: a whole 2x2x4 slice. The times are simulated.
32 devices in a mesh: dp: 2 (over x), tensor: 4 (over z), fsdp: 4 (over y, core).
Axes of the slice: x: 2, y: 2, z: 4, core: 2. Of those that a mesh axis runs over, the one named last changes fastest.
Arguments:
- train_acts: bfloat16 [2048, 4096], P(('dp', 'fsdp'), 'tensor'), may hold values from -6 to 6
- val_acts: bfloat16 [2048, 4096], P(('dp', 'fsdp'), 'tensor'), may hold values from -6 to 6
- train_cot: bfloat16 [2048, 4096], P(('dp', 'fsdp'), 'tensor'), may hold values from -6 to 6
- val_cot: bfloat16 [2048, 4096], P(('dp', 'fsdp'), 'tensor'), may hold values from -6 to 6
- train_lengths: int32 [32], P(('dp', 'fsdp')), may hold values from 16 to 64
- val_lengths: int32 [32], P(('dp', 'fsdp')), may hold values from 16 to 64
- gate_weight: bfloat16 [4096, 11008], P(('dp', 'fsdp'), 'tensor'), may hold values from -0.09375 to 0.09375
- up_weight: bfloat16 [4096, 11008], P(('dp', 'fsdp'), 'tensor'), may hold values from -0.09375 to 0.09375
- in_basis: bfloat16 [11008, 64], P('tensor'), may hold values from -0.0546875 to 0.0546875
- out_basis: bfloat16 [4096, 128], P('tensor'), may hold values from -0.09375 to 0.09375
Outputs:
- scores: float32 [32, 32], P(('dp', 'fsdp'))
Inputs may be any that keep to these rules, and one draw needn't show every extreme that they name: `train_lengths`: an example's first length slots hold its tokens, the rest are padding. `val_lengths`: as for the training examples.
All inputs are finite; a program needn't handle non-finite values.
Results may differ from a plain program's by a relative error of at most 0.004.
Values may be sent and summed in bfloat16 or wider, within the bound.
No kernel may reach another device: no remote copies, remote signals or barrier semaphores. Data moves between devices by JAX's collectives and lax.ppermute only.
A program may use at most 128 MiB of HBM per device.

v0:
```python
import jax
import jax.numpy as jnp
from jax import lax
from jax.sharding import PartitionSpec as P

SEQ = 64


def outer_sums(in_proj, out_proj, valid):
    in_three = in_proj.reshape(valid.shape[0], valid.shape[1], in_proj.shape[1]) * valid[:, :, None]
    out_three = out_proj.reshape(valid.shape[0], valid.shape[1], out_proj.shape[1])
    return jnp.einsum("esj,esk->ejk", in_three, out_three, precision=lax.Precision.HIGHEST)


def on_device(
    train_acts,
    val_acts,
    train_cot,
    val_cot,
    train_lengths,
    val_lengths,
    gate_weight,
    up_weight,
    in_basis,
    out_basis,
):
    train_full, val_full = (
        lax.all_gather(train_acts, "tensor", axis=1, tiled=True),
        lax.all_gather(val_acts, "tensor", axis=1, tiled=True),
    )
    activations = jnp.concatenate([train_full, val_full], axis=0)
    cotangents = jnp.concatenate([train_cot, val_cot], axis=0)
    gate_sum = jnp.dot(
        activations,
        lax.all_gather(gate_weight, ("dp", "fsdp"), axis=0, tiled=True),
        preferred_element_type=jnp.float32,
    )
    up_sum = jnp.dot(
        activations,
        lax.all_gather(up_weight, ("dp", "fsdp"), axis=0, tiled=True),
        preferred_element_type=jnp.float32,
    )
    hidden = (jax.nn.silu(gate_sum) * up_sum).astype(jnp.bfloat16)
    in_part = jnp.dot(hidden, in_basis, preferred_element_type=jnp.float32)
    out_part = jnp.dot(cotangents, out_basis, preferred_element_type=jnp.float32)
    lengths = jnp.concatenate([train_lengths, val_lengths], axis=0)
    valid = (jnp.arange(SEQ, dtype=jnp.int32)[None, :] < lengths[:, None]).astype(jnp.float32)
    in_proj, out_proj = lax.psum((in_part, out_part), "tensor")
    sketch = outer_sums(in_proj, out_proj, valid)
    flat_sketch = sketch.reshape(sketch.shape[0], sketch.shape[1] * sketch.shape[2])
    unit_rows = flat_sketch * lax.rsqrt(
        jnp.sum(flat_sketch * flat_sketch, axis=1, keepdims=True) + 1e-06
    )
    train_count = train_lengths.shape[0]
    train_unit = unit_rows[:train_count]
    val_local = unit_rows[train_count:]
    width_all = flat_sketch.shape[1]
    share = width_all // lax.axis_size("tensor")
    first = lax.axis_index("tensor") * share
    train_share = lax.dynamic_slice_in_dim(train_unit, first, share, 1)
    val_share_local = lax.dynamic_slice_in_dim(val_local, first, share, 1)
    val_share = lax.all_gather(val_share_local, ("dp", "fsdp"), axis=0, tiled=True)
    partial_scores = jnp.dot(
        train_share,
        val_share.T,
        precision=lax.Precision.HIGHEST,
        preferred_element_type=jnp.float32,
    )
    product = lax.psum(partial_scores, "tensor")
    return product * jnp.sqrt(jnp.float32(width_all))


def solution(mesh):
    placed = (
        P(("dp", "fsdp"), "tensor"),
        P(("dp", "fsdp"), "tensor"),
        P(("dp", "fsdp"), "tensor"),
        P(("dp", "fsdp"), "tensor"),
        P(("dp", "fsdp")),
        P(("dp", "fsdp")),
        P(("dp", "fsdp"), "tensor"),
        P(("dp", "fsdp"), "tensor"),
        P("tensor", None),
        P("tensor", None),
    )
    return jax.shard_map(
        on_device, mesh=mesh, in_specs=placed, out_specs=P(("dp", "fsdp"), None), check_vma=False
    )
```

profile of v0, /device:TPU:0, one launch (start us, length us, event | category | flops | bytes accessed | tf_op | source)
XLA Modules:
  0.0 431.9 jit_solution(13203272675145067068)
XLA Ops:
  6.5 0.0 copy-start
  6.5 0.0 copy-start.2
  6.5 0.0 copy-start.1
  6.5 0.0 copy-start.3
  6.5 0.0 all-gather.6.cloned.1.call-start
  6.6 0.7 all-gather.6.cloned.1.call-update
  7.3 0.0 all-gather.8.cloned.1.call-start
  7.3 0.7 all-gather.8.cloned.1.call-update
  8.0 0.0 all-gather.10.cloned.1.call-start
  8.1 0.7 all-gather.10.cloned.1.call-update
  8.8 0.0 all-gather.12.cloned.1.call-start
  8.8 0.5 all-gather.12.cloned.1.call-update
  9.3 0.0 all-reduce.3.cloned.1.call-start
  9.4 0.0 copy-done.2
  9.4 0.0 copy-done.1
  9.4 0.0 copy-done.3
  9.4 1.1 fusion.1
  10.6 46.8 %all-gather.6.cloned.1.call-done = bf16[256,4096]{1,0:T(8,128)(2,1)} async-done(((bf16[256,1024]{1,0:T(8,128)(2,1)}), bf16[256,4096]{1,0:T(8,128)(2,1)}) %all-gather.6.cloned.1.call-update) | async-done | bytes 2097168 | tf_op jit(solution)/shard_map/all_gather | solution.py:28
  57.3 3.1 constant_dynamic-update-slice_fusion.1
  60.4 42.9 %all-gather.8.cloned.1.call-done = bf16[256,4096]{1,0:T(8,128)(2,1)} async-done(((bf16[256,1024]{1,0:T(8,128)(2,1)}), bf16[256,4096]{1,0:T(8,128)(2,1)}) %all-gather.8.cloned.1.call-update) | async-done | bytes 2097168 | tf_op jit(solution)/shard_map/all_gather | solution.py:29
  103.4 3.1 constant_dynamic-update-slice_fusion
  106.5 116.1 %all-gather.10.cloned.1.call-done = bf16[4096,2752]{0,1:T(8,128)(2,1)} async-done(((bf16[512,2752]{0,1:T(8,128)(2,1)}), bf16[4096,2752]{0,1:T(8,128)(2,1)}) %all-gather.10.cloned.1.call-update) | async-done | bytes 22544400 | tf_op jit(solution)/shard_map/all_gather | solution.py:35
  222.7 19.2 %fusion.15 = f32[512,2752]{0,1:T(8,128)} fusion(bf16[512,4096]{1,0:T(8,128)(2,1)} %constant_dynamic-update-slice_fusion, bf16[4096,2752]{0,1:T(8,128)(2,1)} %all-gather.10.cloned.1.call-done), kind=kOutput, calls=%fused_computation.25 | convolution fusion | flops 11542724608 | bytes 32374784 | tf_op jit(solution)/shard_map/dot_general | solution.py:33
  241.9 0.0 copy-start.4
  241.9 0.0 copy-start.5
  241.9 101.1 %all-gather.12.cloned.1.call-done = bf16[4096,2752]{0,1:T(8,128)(2,1)} async-done(((bf16[512,2752]{0,1:T(8,128)(2,1)}), bf16[4096,2752]{0,1:T(8,128)(2,1)}) %all-gather.12.cloned.1.call-update) | async-done | bytes 22544400 | tf_op jit(solution)/shard_map/all_gather | solution.py:40
  343.0 0.0 copy-done
  343.0 20.0 %fusion = f32[512,64]{0,1:T(8,128)S(1)} fusion(bf16[2752,64]{0,1:T(8,128)(2,1)S(1)} %copy-done, f32[512,2752]{0,1:T(8,128)} %fusion.15, bf16[512,4096]{1,0:T(8,128)(2,1)} %constant_dynamic-update-slice_fusion, bf16[4096,2752]{0,1:T(8,128)(2,1)} %all-gather.12.cloned.1.call-done), kind=kOutput, calls=%fused_computation.1 | convolution fusion | flops 11731533824 | bytes 32858112 | tf_op jit(solution)/shard_map/dot_general | solution.py:44
  363.1 0.1 reshape.37
  363.2 0.8 copy.12
  363.9 0.0 all-reduce.3.cloned.1.call-update
  363.9 0.0 copy-done.4
  364.0 0.0 copy-done.5
  364.0 0.1 pad_add_fusion
  364.0 0.1 fusion.10
  364.1 38.7 %all-reduce.3.cloned.1.call-done = (f32[8,64,128]{2,1,0:T(8,128)}, f32[8,64,64]{1,2,0:T(8,128)}) async-done(((f32[8,64,128]{2,1,0:T(8,128)}, f32[8,64,64]{1,2,0:T(8,128)}), (f32[8,64,128]{2,1,0:T(8,128)}, f32[8,64,64]{1,2,0:T(8,128)})) %all-reduce.3.cloned.1.call-update) | async-done | bytes 393232 | tf_op jit(solution)/shard_map/psum | solution.py:48
  402.8 1.5 multiply_reduce_fusion
  404.3 0.2 bitcast_multiply_fusion
  404.6 9.3 %all-gather = f32[8,4,2048]{2,1,0:T(4,128)S(1)} all-gather(f32[1,4,2048]{2,1,0:T(4,128)S(1)} %dynamic-slice_bitcast_fusion), channel_id=1, replica_groups=mesh['dp'=2,'tensor'=4,'fsdp'=4] {'dp','fsdp'}, dimensions={0}, use_global_device_ids=true | all-gather | bytes 294912 | tf_op jit(solution)/shard_map/all_gather | solution.py:62
  413.8 0.1 reshape.41
  413.9 0.3 fusion.8
  414.2 10.6 %psum.23 = f32[4,32]{1,0:T(4,128)S(1)} all-reduce(f32[4,32]{1,0:T(4,128)S(1)} %fusion.8), channel_id=1, replica_groups=mesh['dp'=2,'tensor'=4,'fsdp'=4] {'tensor'}, use_global_device_ids=true, to_apply=%region_3.4 | all-reduce | flops 128 | bytes 1024 | tf_op jit(solution)/shard_map/psum | solution.py:69
  424.8 0.6 broadcast_multiply_fusion
  (3 shorter events, 0.1 us)
Async XLA Ops:
  6.5 336.5 %copy-start = (bf16[2752,64]{0,1:T(8,128)(2,1)S(1)}, bf16[2752,64]{0,1:T(8,128)(2,1)}, u32[]{:S(2)}) copy-start(bf16[2752,64]{0,1:T(8,128)(2,1)} %param.18) | copy-start | bytes 1056772
  6.5 2.8 copy-start.2
  6.5 2.9 copy-start.1
  6.5 2.9 copy-start.3
  6.5 50.8 %all-gather.6.cloned.1.call-start = ((), (), s32[]{:S(2)}) async-start(), calls=%async_computation | async-start | bytes 2621440 | tf_op jit(solution)/shard_map/all_gather | solution.py:28
  7.3 96.1 %all-gather.8.cloned.1.call-start = ((), (), s32[]{:S(2)}) async-start(), calls=%async_computation.1 | async-start | bytes 2621440 | tf_op jit(solution)/shard_map/all_gather | solution.py:29
  8.0 214.7 %all-gather.10.cloned.1.call-start = ((), (), s32[]{:S(2)}) async-start(), calls=%async_computation.2 | async-start | bytes 25362432 | tf_op jit(solution)/shard_map/all_gather | solution.py:35
  8.8 334.3 %all-gather.12.cloned.1.call-start = ((), (), s32[]{:S(2)}) async-start(), calls=%async_computation.3 | async-start | bytes 25362432 | tf_op jit(solution)/shard_map/all_gather | solution.py:40
  9.3 393.4 %all-reduce.3.cloned.1.call-start = ((), (), s32[]{:S(2)}) async-start(), calls=%async_computation.4 | async-start | bytes 1048576 | tf_op jit(solution)/shard_map/psum | solution.py:48
  241.9 122.1 %copy-start.4 = (s32[4]{0:T(128)S(1)}, s32[4]{0:T(128)}, u32[]{:S(2)}) copy-start(s32[4]{0:T(128)} %param.15) | copy-start | bytes 52
  241.9 122.1 %copy-start.5 = (s32[4]{0:T(128)S(1)}, s32[4]{0:T(128)}, u32[]{:S(2)}) copy-start(s32[4]{0:T(128)} %param.14) | copy-start | bytes 52
Sparse Core Ops, SparseCore 0:
  8.9 48.3 all-gather.5
  58.9 44.4 all-gather.7
  105.3 117.3 all-gather.9
  224.4 118.5 all-gather.11
  364.1 38.6 all-reduce.2
where the time goes:
time: 432 us
  waiting for transfers between devices  348 us (81%)
  matrix products  42.2 us (10%)
  blocking collectives  19.9 us (5%)
  between operations  13.2 us (3%)
  local copies, waits for them, and re-layouts  7.28 us (2%)
    all_gather x1, waiting for transfers between devices, on_device(): lax.all_gather(gate_weight, ('dp', 'fsdp'), axis=0, tiled=True)  116 us
    all_gather x1, waiting for transfers between devices, on_device(): lax.all_gather(up_weight, ('dp', 'fsdp'), axis=0, tiled=True)  101 us
    all_gather x1, waiting for transfers between devices, on_device(): lax.all_gather(train_acts, 'tensor', axis=1, tiled=True)  46.8 us
    all_gather x1, waiting for transfers between devices, on_device(): lax.all_gather(val_acts, 'tensor', axis=1, tiled=True)  42.9 us
    psum x1, waiting for transfers between devices, on_device(): in_proj, out_proj = lax.psum((in_part, out_part), 'tensor')  38.7 us
    dot_general x1, matrix products, on_device(): in_part = jnp.dot(hidden, in_basis, preferred_element_type=jnp.float32)  20 us
    dot_general x1, matrix products, on_device(): jnp.dot(activations, lax.all_gather(gate_weight, ('dp', 'fsdp'), axis=0,...  19.2 us
    psum x1, blocking collectives, on_device(): product = lax.psum(partial_scores, 'tensor')  10.6 us
  transfers between devices with their start and end apart: 5, of which 5 were waited for; matrix products, arithmetic and copies ran while one was open for 6% of the time, Pallas kernels for 0%

commit v1 on v0

--- a/solution.py
+++ b/solution.py
@@ -4,6 +4,19 @@
 from jax.sharding import PartitionSpec as P
 
 SEQ = 64
+
+
+def ring_gather(x, axis, dim):
+    ways = lax.axis_size(axis)
+    up = [(d, (d + 1) % ways) for d in range(ways)]
+    down = [(d, (d - 1) % ways) for d in range(ways)]
+    earlier, later = ([x], [x])
+    for _ in range(ways // 2):
+        earlier.append(lax.ppermute(earlier[-1], axis, up))
+    for _ in range((ways - 1) // 2):
+        later.append(lax.ppermute(later[-1], axis, down))
+    line = jnp.concatenate([*earlier[::-1], *later[1:]], axis=dim)
+    return jnp.roll(line, (lax.axis_index(axis) - ways // 2) * x.shape[dim], axis=dim)
 
 
 def outer_sums(in_proj, out_proj, valid):
@@ -36,9 +49,7 @@
         preferred_element_type=jnp.float32,
     )
     up_sum = jnp.dot(
-        activations,
-        lax.all_gather(up_weight, ("dp", "fsdp"), axis=0, tiled=True),
-        preferred_element_type=jnp.float32,
+        activations, ring_gather(up_weight, ("dp", "fsdp"), 0), preferred_element_type=jnp.float32
     )
     hidden = (jax.nn.silu(gate_sum) * up_sum).astype(jnp.bfloat16)
     in_part = jnp.dot(hidden, in_basis, preferred_element_type=jnp.float32)

time: 432 us -> 474 us (1.097)
  waiting for transfers between devices: 348 us -> 210 us
  starting transfers between devices: 0.18 us -> 135 us
  local copies, waits for them, and re-layouts: 7.28 us -> 52 us
    ppermute x0 -> x7, starting transfers between devices: none -> 134 us  [the longest x4 132 us: ring_gather(): earlier.append(lax.ppermute(earlier[-1], axis, up))]
    ppermute x0 -> x7, waiting for transfers between devices: none -> 128 us  [the longest x4 72.1 us: ring_gather(): earlier.append(lax.ppermute(earlier[-1], axis, up))]
    all_gather x1, waiting for transfers between devices: 116 us -> 0.01 us  [on_device(): lax.all_gather(gate_weight, ('dp', 'fsdp'), axis=0, tiled=True)]
    all_gather x1 -> x0, waiting for transfers between devices: 101 us -> none  [on_device(): lax.all_gather(up_weight, ('dp', 'fsdp'), axis=0, tiled=True)]
    all_gather x1, waiting for transfers between devices: 46.8 us -> 0.01 us  [on_device(): lax.all_gather(train_acts, 'tensor', axis=1, tiled=True)]
    unnamed x15 -> x30, local copies, waits for them, and re-layouts: 3.24 us -> 46.2 us
    all_gather x1, waiting for transfers between devices: 42.9 us -> 0.01 us  [on_device(): lax.all_gather(val_acts, 'tensor', axis=1, tiled=True)]
    psum x1, waiting for transfers between devices: 38.7 us -> 80.1 us  [on_device(): in_proj, out_proj = lax.psum((in_part, out_part), 'tensor')]
  transfers between devices with their start and end apart: 5 -> 11, of which waited for: 5 -> 5; matrix products, arithmetic and copies ran while one was open for 6% -> 11% of each run, Pallas kernels for 0% -> 0%
where the time goes in v1:
time: 474 us
  waiting for transfers between devices  210 us (44%)
  starting transfers between devices  135 us (28%)
  local copies, waits for them, and re-layouts  52 us (11%)
  matrix products  43.3 us (9%)
  blocking collectives  19.9 us (4%)
  between operations  13.2 us (3%)
    ppermute x4, starting transfers between devices, ring_gather(): earlier.append(lax.ppermute(earlier[-1], axis, up))  132 us
    psum x1, waiting for transfers between devices, on_device(): in_proj, out_proj = lax.psum((in_part, out_part), 'tensor')  80.1 us
    ppermute x4, waiting for transfers between devices, ring_gather(): earlier.append(lax.ppermute(earlier[-1], axis, up))  72.1 us
    ppermute x3, waiting for transfers between devices, ring_gather(): later.append(lax.ppermute(later[-1], axis, down))  55.6 us
    unnamed x30, local copies, waits for them, and re-layouts  46.2 us
    dot_general x1, matrix products, on_device(): in_part = jnp.dot(hidden, in_basis, preferred_element_type=jnp.float32)  20.1 us
    dot_general x1, matrix products, on_device(): jnp.dot(activations, lax.all_gather(gate_weight, ('dp', 'fsdp'), axis=0,...  19.1 us
    psum x1, blocking collectives, on_device(): product = lax.psum(partial_scores, 'tensor')  10.6 us
  transfers between devices with their start and end apart: 11, of which 5 were waited for; matrix products, arithmetic and copies ran while one was open for 11% of the time, Pallas kernels for 0%

profile of v1, /device:TPU:0, one launch (start us, length us, event | category | flops | bytes accessed | tf_op | source)
XLA Modules:
  0.0 473.8 jit_solution(13475752835851372447)
XLA Ops:
  6.5 0.0 copy-start
  6.5 0.0 all-gather.5.cloned.1.call-start
  6.5 0.7 all-gather.5.cloned.1.call-update
  7.3 0.0 all-gather.7.cloned.1.call-start
  7.3 0.7 all-gather.7.cloned.1.call-update
  8.0 0.0 all-gather.9.cloned.1.call-start
  8.1 0.7 all-gather.9.cloned.1.call-update
  8.7 0.0 all-reduce.3.cloned.1.call-start
  8.8 0.5 collective-permute-start
  9.3 34.5 %collective-permute-done = bf16[512,2752]{0,1:T(8,128)(2,1)S(1)} collective-permute-done((bf16[512,2752]{0,1:T(8,128)(2,1)}, bf16[512,2752]{0,1:T(8,128)(2,1)S(1)}, u32[]{:S(2)}, u32[]{:S(2)}) %collective-permute-start) | collective-permute-done | bytes 2818080 | tf_op jit(solution)/shard_map/ppermute | solution.py:15
  43.9 0.0 collective-permute-start.1
  43.9 2.6 collective-permute-start.4
  46.5 31.5 %collective-permute-done.1 = bf16[512,2752]{0,1:T(8,128)(2,1)S(1)} collective-permute-done((bf16[512,2752]{0,1:T(8,128)(2,1)S(1)}, bf16[512,2752]{0,1:T(8,128)(2,1)S(1)}, u32[]{:S(2)}, u32[]{:S(2)}) %collective-permute-start.1) | collective-permute-done | bytes 2818080 | tf_op jit(solution)/shard_map/ppermute | solution.py:15
  78.0 0.0 copy-start.2
  78.0 1.6 copy-done.2
  79.6 28.2 %collective-permute-start.2 = (bf16[512,2752]{0,1:T(8,128)(2,1)S(1)}, bf16[512,2752]{0,1:T(8,128)(2,1)}, u32[]{:S(2)}, u32[]{:S(2)}) collective-permute-start(bf16[512,2752]{0,1:T(8,128)(2,1)S(1)} %collective-permute-done.1), channel_id=1, source_target_pairs={{0,1},{1,2},{2,3},{3,16},{16,17},{17,18},{18,19},{19,0},{4,5},{5,6... | collective-permute-start | bytes 8454152 | tf_op jit(solution)/shard_map/ppermute | solution.py:15
  107.8 0.0 collective-permute-done.4
  107.8 0.0 collective-permute-start.5
  107.8 6.1 %collective-permute-done.2 = bf16[512,2752]{0,1:T(8,128)(2,1)} collective-permute-done((bf16[512,2752]{0,1:T(8,128)(2,1)S(1)}, bf16[512,2752]{0,1:T(8,128)(2,1)}, u32[]{:S(2)}, u32[]{:S(2)}) %collective-permute-start.2) | collective-permute-done | bytes 2818080 | tf_op jit(solution)/shard_map/ppermute | solution.py:15
  113.9 103.0 %collective-permute-start.3 = (bf16[512,2752]{0,1:T(8,128)(2,1)}, bf16[512,2752]{0,1:T(8,128)(2,1)}, u32[]{:S(2)}, u32[]{:S(2)}) collective-permute-start(bf16[512,2752]{0,1:T(8,128)(2,1)} %collective-permute-done.2), channel_id=1, source_target_pairs={{0,1},{1,2},{2,3},{3,16},{16,17},{17,18},{18,19},{19,0},{4,5},{5,6... | collective-permute-start | bytes 8454152 | tf_op jit(solution)/shard_map/ppermute | solution.py:15
  216.9 2.4 fusion.8
  219.3 0.0 all-gather.5.cloned.1.call-done
  219.3 3.1 constant_dynamic-update-slice_fusion.1
  222.5 3.1 constant_dynamic-update-slice_fusion
  225.6 0.0 collective-permute-done.5
  225.6 0.0 collective-permute-start.6
  225.6 0.0 collective-permute-done.3
  225.6 3.7 constant_dynamic-update-slice_fusion.17
  229.3 3.6 constant_dynamic-update-slice_fusion.16
  232.9 0.0 copy-done.3
  232.9 1.8 constant_dynamic-update-slice_fusion.15
  234.7 1.8 constant_dynamic-update-slice_fusion.14
  236.4 0.0 copy-done.1
  236.4 1.8 constant_dynamic-update-slice_fusion.13
  238.2 3.6 constant_dynamic-update-slice_fusion.12
  241.8 3.6 constant_dynamic-update-slice_fusion.11
  245.4 55.6 %collective-permute-done.6 = bf16[512,2752]{0,1:T(8,128)(2,1)S(1)} collective-permute-done((bf16[512,2752]{0,1:T(8,128)(2,1)}, bf16[512,2752]{0,1:T(8,128)(2,1)S(1)}, u32[]{:S(2)}, u32[]{:S(2)}) %collective-permute-start.6) | collective-permute-done | bytes 2818080 | tf_op jit(solution)/shard_map/ppermute | solution.py:17
  301.0 1.9 constant_dynamic-update-slice_fusion.10
  302.9 3.7 constant_dynamic-update-slice_fusion.9
  306.5 3.7 constant_dynamic-update-slice_fusion.8
  310.2 1.8 constant_dynamic-update-slice_fusion.7
  312.0 1.8 constant_dynamic-update-slice_fusion.6
  313.7 1.7 constant_dynamic-update-slice_fusion.5
  315.5 3.6 constant_dynamic-update-slice_fusion.4
  319.1 3.5 constant_dynamic-update-slice_fusion.3
  322.6 1.7 constant_dynamic-update-slice_fusion.2
  324.3 19.1 %fusion.24 = f32[512,2752]{0,1:T(8,128)} fusion(bf16[512,4096]{1,0:T(8,128)(2,1)} %constant_dynamic-update-slice_fusion, bf16[4096,2752]{0,1:T(8,128)(2,1)} %all-gather.9.cloned.1.call-done), kind=kOutput, calls=%fused_computation.45 | convolution fusion | flops 11542724608 | bytes 32374784 | tf_op jit(solution)/shard_map/dot_general | solution.py:46
  343.4 0.0 copy-done
  343.4 20.1 %fusion.5 = f32[512,64]{0,1:T(8,128)S(1)} fusion(bf16[2752,64]{0,1:T(8,128)(2,1)S(1)} %copy-done, f32[512,2752]{0,1:T(8,128)} %fusion.24, bf16[512,4096]{1,0:T(8,128)(2,1)} %constant_dynamic-update-slice_fusion, bf16[8192,2752]{0,1:T(8,128)(2,1)} %constant_dynamic-update-slice_fusion.2, s32[]{:T(128)S(6)} %select_n.18), kind=kOutput, calls=%fused_computation.3 | convolution fusion | flops 11731533824 | bytes 32858116 | tf_op jit(solution)/shard_map/dot_general | solution.py:55
  363.5 0.1 reshape.37
  363.6 0.8 copy.12
  364.4 0.0 all-reduce.3.cloned.1.call-update
  364.4 0.0 copy-done.4
  364.4 0.0 copy-done.5
  364.4 0.1 pad_add_fusion
  364.5 0.1 fusion.17
  364.6 80.1 %all-reduce.3.cloned.1.call-done = (f32[8,64,128]{2,1,0:T(8,128)}, f32[8,64,64]{1,2,0:T(8,128)}) async-done(((f32[8,64,128]{2,1,0:T(8,128)}, f32[8,64,64]{1,2,0:T(8,128)}), (f32[8,64,128]{2,1,0:T(8,128)}, f32[8,64,64]{1,2,0:T(8,128)})) %all-reduce.3.cloned.1.call-update) | async-done | bytes 393232 | tf_op jit(solution)/shard_map/psum | solution.py:59
  444.6 1.5 multiply_reduce_fusion
  446.2 0.2 bitcast_multiply_fusion
  446.4 9.3 %all-gather = f32[8,4,2048]{2,1,0:T(4,128)S(1)} all-gather(f32[1,4,2048]{2,1,0:T(4,128)S(1)} %dynamic-slice_bitcast_fusion), channel_id=1, replica_groups=mesh['dp'=2,'tensor'=4,'fsdp'=4] {'dp','fsdp'}, dimensions={0}, use_global_device_ids=true | all-gather | bytes 294912 | tf_op jit(solution)/shard_map/all_gather | solution.py:73
  455.7 0.1 reshape.41
  455.8 0.3 fusion.15
  456.0 10.6 %psum.23 = f32[4,32]{1,0:T(4,128)S(1)} all-reduce(f32[4,32]{1,0:T(4,128)S(1)} %fusion.15), channel_id=1, replica_groups=mesh['dp'=2,'tensor'=4,'fsdp'=4] {'tensor'}, use_global_device_ids=true, to_apply=%region_3.4 | all-reduce | flops 128 | bytes 1024 | tf_op jit(solution)/shard_map/psum | solution.py:80
  466.7 0.6 broadcast_multiply_fusion
  (9 shorter events, 0.1 us)
Async XLA Ops:
  6.5 336.9 %copy-start = (bf16[2752,64]{0,1:T(8,128)(2,1)S(1)}, bf16[2752,64]{0,1:T(8,128)(2,1)}, u32[]{:S(2)}) copy-start(bf16[2752,64]{0,1:T(8,128)(2,1)} %param.18) | copy-start | bytes 1056772
  6.5 212.8 %all-gather.5.cloned.1.call-start = ((), (), s32[]{:S(2)}) async-start(), calls=%async_computation | async-start | bytes 2621440 | tf_op jit(solution)/shard_map/all_gather | solution.py:41
  7.3 215.2 %all-gather.7.cloned.1.call-start = ((), (), s32[]{:S(2)}) async-start(), calls=%async_computation.1 | async-start | bytes 2621440 | tf_op jit(solution)/shard_map/all_gather | solution.py:42
  8.0 316.3 %all-gather.9.cloned.1.call-start = ((), (), s32[]{:S(2)}) async-start(), calls=%async_computation.2 | async-start | bytes 25362432 | tf_op jit(solution)/shard_map/all_gather | solution.py:48
  8.7 435.9 %all-reduce.3.cloned.1.call-start = ((), (), s32[]{:S(2)}) async-start(), calls=%async_computation.3 | async-start | bytes 1048576 | tf_op jit(solution)/shard_map/psum | solution.py:59
  8.8 35.1 %collective-permute-start = (bf16[512,2752]{0,1:T(8,128)(2,1)}, bf16[512,2752]{0,1:T(8,128)(2,1)S(1)}, u32[]{:S(2)}, u32[]{:S(2)}) collective-permute-start(bf16[512,2752]{0,1:T(8,128)(2,1)} %param.17), channel_id=1, source_target_pairs={{0,1},{1,2},{2,3},{3,16},{16,17},{17,18},{18,19},{19,0},{4,5},{5,6... | collective-permute-start | bytes 8454152 | tf_op jit(solution)/shard_map/ppermute | solution.py:15
  43.9 34.2 %collective-permute-start.1 = (bf16[512,2752]{0,1:T(8,128)(2,1)S(1)}, bf16[512,2752]{0,1:T(8,128)(2,1)S(1)}, u32[]{:S(2)}, u32[]{:S(2)}) collective-permute-start(bf16[512,2752]{0,1:T(8,128)(2,1)S(1)} %collective-permute-done), channel_id=1, source_target_pairs={{0,1},{1,2},{2,3},{3,16},{16,17},{17,18},{18,19},{19,0},{4,5},{5,6... | collective-permute-start | bytes 8454152 | tf_op jit(solution)/shard_map/ppermute | solution.py:15
  43.9 64.0 %collective-permute-start.4 = (bf16[512,2752]{0,1:T(8,128)(2,1)}, bf16[512,2752]{0,1:T(8,128)(2,1)}, u32[]{:S(2)}, u32[]{:S(2)}) collective-permute-start(bf16[512,2752]{0,1:T(8,128)(2,1)} %param.17), channel_id=1, source_target_pairs={{0,19},{1,0},{2,1},{3,2},{16,3},{17,16},{18,17},{19,18},{4,23},{5,... | collective-permute-start | bytes 8454152 | tf_op jit(solution)/shard_map/ppermute | solution.py:17
  78.0 1.6 copy-start.2
  79.6 34.3 %collective-permute-start.2 = (bf16[512,2752]{0,1:T(8,128)(2,1)S(1)}, bf16[512,2752]{0,1:T(8,128)(2,1)}, u32[]{:S(2)}, u32[]{:S(2)}) collective-permute-start(bf16[512,2752]{0,1:T(8,128)(2,1)S(1)} %collective-permute-done.1), channel_id=1, source_target_pairs={{0,1},{1,2},{2,3},{3,16},{16,17},{17,18},{18,19},{19,0},{4,5},{5,6... | collective-permute-start | bytes 8454152 | tf_op jit(solution)/shard_map/ppermute | solution.py:15
  107.8 117.8 %collective-permute-start.5 = (bf16[512,2752]{0,1:T(8,128)(2,1)}, bf16[512,2752]{0,1:T(8,128)(2,1)}, u32[]{:S(2)}, u32[]{:S(2)}) collective-permute-start(bf16[512,2752]{0,1:T(8,128)(2,1)} %collective-permute-done.4), channel_id=1, source_target_pairs={{0,19},{1,0},{2,1},{3,2},{16,3},{17,16},{18,17},{19,18},{4,23},{5,... | collective-permute-start | bytes 8454152 | tf_op jit(solution)/shard_map/ppermute | solution.py:17
  113.9 111.7 %collective-permute-start.3 = (bf16[512,2752]{0,1:T(8,128)(2,1)}, bf16[512,2752]{0,1:T(8,128)(2,1)}, u32[]{:S(2)}, u32[]{:S(2)}) collective-permute-start(bf16[512,2752]{0,1:T(8,128)(2,1)} %collective-permute-done.2), channel_id=1, source_target_pairs={{0,1},{1,2},{2,3},{3,16},{16,17},{17,18},{18,19},{19,0},{4,5},{5,6... | collective-permute-start | bytes 8454152 | tf_op jit(solution)/shard_map/ppermute | solution.py:15
  225.6 7.3 %copy-start.3 = (bf16[512,2752]{0,1:T(8,128)(2,1)S(1)}, bf16[512,2752]{0,1:T(8,128)(2,1)}, u32[]{:S(2)}) copy-start(bf16[512,2752]{0,1:T(8,128)(2,1)} %copy-done.2) | copy-start | bytes 8454148
  225.6 75.4 %collective-permute-start.6 = (bf16[512,2752]{0,1:T(8,128)(2,1)}, bf16[512,2752]{0,1:T(8,128)(2,1)S(1)}, u32[]{:S(2)}, u32[]{:S(2)}) collective-permute-start(bf16[512,2752]{0,1:T(8,128)(2,1)} %collective-permute-done.5), channel_id=1, source_target_pairs={{0,19},{1,0},{2,1},{3,2},{16,3},{17,16},{18,17},{19,18},{4,23},{5,... | collective-permute-start | bytes 8454152 | tf_op jit(solution)/shard_map/ppermute | solution.py:17
  232.9 3.6 copy-start.1
  343.4 21.0 %copy-start.4 = (s32[4]{0:T(128)S(1)}, s32[4]{0:T(128)}, u32[]{:S(2)}) copy-start(s32[4]{0:T(128)} %param.15) | copy-start | bytes 52
  343.4 21.0 %copy-start.5 = (s32[4]{0:T(128)S(1)}, s32[4]{0:T(128)}, u32[]{:S(2)}) copy-start(s32[4]{0:T(128)} %param.14) | copy-start | bytes 52
Sparse Core Ops, SparseCore 0:
  8.9 48.3 all-gather.4
  58.9 44.4 all-gather.6
  105.3 206.4 all-gather.8
  364.5 80.0 all-reduce.2
